TPU v7x, 32 devices: a whole 2x2x4 slice. The times are simulated.
32 devices in a mesh: rec: 4 (over y, core), tm: 8 (over z, x).
Axes of the slice: x: 2, y: 2, z: 4, core: 2. Of those that a mesh axis runs over, the one named last changes fastest.
Arguments:
- frames: bfloat16 [4, 4096, 1024], P('rec', 'tm'), may hold values from -6 to 6
- lengths: int32 [4], P('rec'), may hold values from 1024 to 4096, as said below
- norm_gain: float32 [1024], replicated, may hold values from 0.1 to 1.9
- memory_gain: float32 [1024], replicated, may hold values from 0.1 to 1.9
- qkv_weight: bfloat16 [3, 1024, 1024], P(None, None, 'tm'), may hold values from -3.75 to 3.75
- out_weight: bfloat16 [1024, 1024], P(None, 'tm'), may hold values from -0.1875 to 0.1875
- segment_ids: int32 [4, 8, 512], P('rec', 'tm'), may hold values from 0 to 127, never falling along the last dimension, each value on 1 to 12 neighbouring positions
- owners: int32 [4, 8, 128, 1], P('rec', 'tm'), may hold values from 0 to 7; in each aligned block of 128 rows (0 to 127, 128 to 255, ..., all dimensions but the last counted through in order) at most 32 rows name the same one
- language_weight: bfloat16 [1024, 2048], P(None, 'rec'), may hold values from -0.1875 to 0.1875
Outputs:
- encoded: bfloat16 [4, 4096, 1024], P('rec', 'tm')
- lm_rows: bfloat16 [4, 8, 256, 2048], P('rec', 'tm')
Inputs may be any that keep to these rules, and one draw needn't show every extreme that they name: `lengths`: one recording has exactly 4096 live frames. `segment_ids`: in each block, token numbers never fall and each of the 128 tokens has 1 to 12 frames, one exactly 12. `owners`: within the 128 tokens of one block no owner is named more than 32 times, a bound that some block reaches.
All inputs are finite; a program needn't handle non-finite values.
Results may differ from a plain program's by a relative error of at most 0.035.
Values may be sent and summed in bfloat16 or wider, within the bound.
No kernel may reach another device: no remote copies, remote signals or barrier semaphores. Data moves between devices by JAX's collectives and lax.ppermute only.
A program may use at most 64 MiB of HBM per device.

v0:
```python
import jax
import jax.numpy as jnp
from jax import lax
from jax.sharding import PartitionSpec as P

H = 16
C = 32
RC = 8
EPS_NORM = 1e-05
EPS_MEMORY = 1e-06
NEG_BIG = -1e30


def shifted(block, axis, distance):
    devices = range(lax.axis_size(axis))
    route = [(i - distance, i) for i in devices if i - distance in devices]
    return lax.ppermute(block, axis, route)


def layer_norm(values_in, gain):
    values_in = values_in.astype(jnp.float32)
    centre = jnp.mean(values_in, axis=-1, keepdims=True)
    centred = values_in - centre
    spread = jnp.mean(centred * centred, axis=-1, keepdims=True)
    return centred * lax.rsqrt(spread + EPS_NORM) * gain


def span_memory(normed, live_mask, gain, span_len):
    model_width = normed.shape[1]
    masked = jnp.where(live_mask[:, None], normed.astype(jnp.float32), jnp.float32(0.0))
    owner_sums = masked.reshape(-1, span_len, model_width).sum(axis=1)
    counts = live_mask.reshape(-1, span_len).astype(jnp.float32).sum(axis=1)
    means = owner_sums / jnp.maximum(counts, 1.0)[:, None]
    power = jnp.mean(means * means, axis=-1, keepdims=True)
    return (means * lax.rsqrt(power + EPS_MEMORY) * gain).astype(jnp.bfloat16)


def block_size():
    return 256


def local_part(query, keys, values, first_frame, length, head_count, span_len, right_len):
    frame_count, model_width = query.shape
    head_size = model_width // head_count
    group_rows = 4 * span_len
    group_count = frame_count // group_rows
    block_rows = block_size()
    query_blocks = query.reshape(group_count, group_rows, head_count, head_size)
    key_blocks = keys[:frame_count].reshape(group_count, group_rows, head_count, head_size)
    value_blocks = values[:frame_count].reshape(group_count, group_rows, head_count, head_size)
    key_tail = keys[frame_count:].reshape(1, right_len, head_count, head_size)
    value_tail = values[frame_count:].reshape(1, right_len, head_count, head_size)
    key_all = jnp.concatenate(
        [key_blocks, jnp.concatenate([key_blocks[1:, :right_len], key_tail], axis=0)], axis=1
    )
    value_all = jnp.concatenate(
        [value_blocks, jnp.concatenate([value_blocks[1:, :right_len], value_tail], axis=0)], axis=1
    )
    start_offsets = jnp.arange(group_count, dtype=jnp.int32)[:, None] * group_rows
    query_pos = first_frame + start_offsets + jnp.arange(group_rows, dtype=jnp.int32)[None, :]
    key_pos = first_frame + jnp.concatenate(
        [
            start_offsets + jnp.arange(group_rows, dtype=jnp.int32)[None, :],
            start_offsets + group_rows + jnp.arange(right_len, dtype=jnp.int32)[None, :],
        ],
        axis=1,
    )
    query_span = query_pos // span_len
    span_end = (query_span + 1) * span_len
    same = (key_pos // span_len)[:, None, :] == query_span[:, :, None]
    ahead = (key_pos[:, None, :] >= span_end[:, :, None]) & (
        key_pos[:, None, :] < span_end[:, :, None] + right_len
    )
    allowed = (same | ahead) & (key_pos < length)[:, None, :]
    scores = jnp.einsum(
        "gqhd,gkhd->ghqk", query_blocks, key_all, preferred_element_type=jnp.float32
    ) * head_size ** (-0.5)
    scores = jnp.where(allowed[:, None], scores, NEG_BIG)
    row_peak = jnp.max(scores, axis=-1)
    weights = jnp.where(allowed[:, None], jnp.exp(scores - row_peak[..., None]), jnp.float32(0.0))
    row_total = jnp.sum(weights, axis=-1)
    accum = jnp.einsum(
        "ghqk,gkhd->ghqd",
        weights.astype(jnp.bfloat16),
        value_all,
        preferred_element_type=jnp.float32,
    )
    block_count = frame_count // block_rows
    row_peak = (
        row_peak.transpose(1, 0, 2).reshape(head_count, block_count, block_rows).transpose(1, 0, 2)
    )
    row_total = (
        row_total.transpose(1, 0, 2).reshape(head_count, block_count, block_rows).transpose(1, 0, 2)
    )
    accum = (
        accum.transpose(1, 0, 2, 3)
        .reshape(head_count, block_count, block_rows, head_size)
        .transpose(1, 0, 2, 3)
    )
    return (row_peak, row_total, accum)


def memory_update(
    carry, memory_keys, memory_values, query, first_frame, length, head_count, span_len
):
    row_peak, row_total, accum = carry
    block_count, _, block_rows = row_peak.shape
    row_count, model_width = memory_keys.shape
    head_size = model_width // head_count
    mem_keys = memory_keys.reshape(row_count, head_count, head_size)
    mem_values = memory_values.reshape(row_count, head_count, head_size)
    mem_index = jnp.arange(row_count, dtype=jnp.int32)
    mem_live = mem_index * span_len < length
    query_blocks = query.reshape(block_count, block_rows, head_count, head_size)
    positions = first_frame + jnp.arange(block_count * block_rows, dtype=jnp.int32).reshape(
        block_count, block_rows
    )

    def one_block(packed):
        query_now, pos_now, peak_now, total_now, accum_now = packed
        scores = jnp.einsum(
            "qhd,khd->hqk", query_now, mem_keys, preferred_element_type=jnp.float32
        ) * head_size ** (-0.5)
        allowed = (mem_index[None, :] < (pos_now // span_len)[:, None]) & mem_live[None, :]
        scores = jnp.where(allowed[None], scores, NEG_BIG)
        new_peak = jnp.maximum(peak_now, jnp.max(scores, axis=-1))
        weights = jnp.where(allowed[None], jnp.exp(scores - new_peak[..., None]), jnp.float32(0.0))
        factor = jnp.exp(peak_now - new_peak)
        total_next = total_now * factor + jnp.sum(weights, axis=-1)
        accum_next = accum_now * factor[..., None] + jnp.einsum(
            "hqk,khd->hqd",
            weights.astype(jnp.bfloat16),
            mem_values,
            preferred_element_type=jnp.float32,
        )
        return (new_peak, total_next, accum_next)

    return lax.map(one_block, (query_blocks, positions, row_peak, row_total, accum))


def finish(carry, frame_count, model_width):
    row_peak, row_total, accum = carry
    result = accum / row_total[..., None]
    return result.transpose(0, 2, 1, 3).reshape(frame_count, model_width).astype(jnp.bfloat16)


def dispatch_matrix(owner_ids, owner_count, capacity):
    choose = (owner_ids[:, None] == jnp.arange(owner_count, dtype=jnp.int32)[None, :]).astype(
        jnp.int32
    )
    before = jnp.cumsum(choose, axis=0) - choose
    slot_index = jnp.sum(before * choose, axis=1)
    target = owner_ids * capacity + slot_index
    slot_rows = jnp.arange(owner_count * capacity, dtype=jnp.int32)
    return (slot_rows[:, None] == target[None, :]).astype(jnp.bfloat16)


def per_device(
    frames,
    lengths,
    norm_gain,
    memory_gain,
    qkv_weight,
    out_weight,
    segment_ids,
    owners,
    language_weight,
):
    local_frames = frames[0]
    frame_count, model_width = local_frames.shape
    head_count = H
    time_count = lax.axis_size("tm")
    first_frame = lax.axis_index("tm") * frame_count
    length = lengths[0]
    live_mask = first_frame + jnp.arange(frame_count, dtype=jnp.int32) < length
    right_frames = shifted(local_frames[:RC], "tm", -1)
    normed = layer_norm(local_frames, norm_gain).astype(jnp.bfloat16)
    normed_right = layer_norm(right_frames, norm_gain).astype(jnp.bfloat16)
    memory = span_memory(normed, live_mask, memory_gain, C)
    stacked_rows = jnp.concatenate([normed, normed_right, memory], axis=0)
    projected = jnp.einsum(
        "fd,kdw->kfw",
        stacked_rows,
        lax.all_gather(qkv_weight, "tm", axis=2, tiled=True),
        preferred_element_type=jnp.float32,
    ).astype(jnp.bfloat16)
    split_at = frame_count + RC
    query = projected[0, :frame_count]
    keys = projected[1, :split_at]
    values = projected[2, :split_at]
    memory_keys = projected[1, split_at:]
    memory_values = projected[2, split_at:]
    carry = local_part(query, keys, values, first_frame, length, head_count, C, RC)
    carry = memory_update(
        carry,
        lax.all_gather(memory_keys, "tm", axis=0, tiled=True),
        lax.all_gather(memory_values, "tm", axis=0, tiled=True),
        query,
        first_frame,
        length,
        head_count,
        C,
    )
    attended = finish(carry, frame_count, model_width)
    output_proj = jnp.dot(
        attended,
        lax.all_gather(out_weight, "tm", axis=1, tiled=True),
        preferred_element_type=jnp.float32,
    )
    encoded = jnp.where(
        live_mask[:, None], local_frames.astype(jnp.float32) + output_proj, jnp.float32(0.0)
    ).astype(jnp.bfloat16)
    token_count = owners.shape[2]
    segments = segment_ids[0, 0]
    owner_indicator = (
        segments[None, :] == jnp.arange(token_count, dtype=jnp.int32)[:, None]
    ).astype(jnp.bfloat16)
    owner_sums = jnp.dot(owner_indicator, encoded, preferred_element_type=jnp.float32)
    counts = jnp.sum(owner_indicator.astype(jnp.float32), axis=1)
    pooled_rows = (owner_sums / counts[:, None]).astype(jnp.bfloat16)
    slot_count = 2 * token_count
    capacity = slot_count // time_count
    route_matrix = dispatch_matrix(owners[0, 0, :, 0], time_count, capacity)
    sent_rows = jnp.dot(route_matrix, pooled_rows, preferred_element_type=jnp.float32).astype(
        jnp.bfloat16
    )
    received = lax.all_to_all(
        sent_rows.reshape(time_count, capacity, model_width),
        "tm",
        split_axis=0,
        concat_axis=0,
        tiled=True,
    )
    received = received.reshape(slot_count, model_width)
    lm_out = jnp.dot(
        received,
        lax.all_gather(language_weight, "rec", axis=1, tiled=True),
        preferred_element_type=jnp.float32,
    ).astype(jnp.bfloat16)
    return (encoded[None], lm_out[None, None])


def solution(mesh):
    in_specs = (
        P("rec", "tm", None),
        P("rec"),
        P(),
        P(),
        P(None, None, "tm"),
        P(None, "tm"),
        P("rec", "tm", None),
        P("rec", "tm", None, None),
        P(None, "rec"),
    )
    out_specs = (P("rec", "tm", None), P("rec", "tm", None, None))
    return jax.shard_map(
        per_device, mesh=mesh, in_specs=in_specs, out_specs=out_specs, check_vma=False
    )
```

profile of v0, /device:TPU:0, one launch (start us, length us, event | category | flops | bytes accessed | tf_op | source)
XLA Modules:
  0.0 270.1 jit_solution(14263593374666861622)
XLA Ops:
  16.4 95.8 %all-gather.6.cloned.1.call-done = bf16[3,1024,1024]{2,1,0:T(8,128)(2,1)} async-done(((bf16[3,1024,128]{2,1,0:T(8,128)(2,1)}), bf16[3,1024,1024]{2,1,0:T(8,128)(2,1)}) %all-gather.6.cloned.1.call-update) | async-done | bytes 6291472 | tf_op jit(solution)/shard_map/all_gather | solution.py:184
  112.3 6.8 %convert_bitcast_fusion = bf16[3,536,1024]{2,1,0:T(8,128)(2,1)S(1)} fusion(bf16[3,1024,1024]{2,1,0:T(8,128)(2,1)} %all-gather.6.cloned.1.call-done, bf16[16,1024]{1,0:T(8,128)(2,1)S(1)} %multiply_convert_fusion.2, bf16[8,1024]{1,0:T(8,128)(2,1)S(1)} %fusion.75, bf16[512,1024]{1,0:T(8,128)(2,1)S(1)} %multiply_convert_fusion.1), kind=kOutput, calls=%fused_computation.46 | convolution fusion | flops 3377160192 | bytes 10682368 | tf_op jit(solution)/shard_map/fd,kdw->kfw/dot_general | solution.py:181
  119.1 1.9 fusion.88
  121.5 2.3 reshape.439
  123.8 2.3 reshape.440
  127.5 3.0 %reshape.441 = bf16[4,128,16,64]{3,2,1,0:T(8,128)(2,1)S(1)} reshape(bf16[1,512,1024]{2,1,0:T(8,128)(2,1)} %get-tuple-element.258) | data formatting | bytes 2097152 | tf_op jit(solution)/shard_map/reshape | solution.py:49
  130.5 2.5 copy.70
  132.9 2.1 slice.56
  135.3 3.0 %reshape.442 = bf16[4,128,16,64]{3,2,1,0:T(8,128)(2,1)S(1)} reshape(bf16[1,512,1024]{2,1,0:T(8,128)(2,1)} %get-tuple-element.257) | data formatting | bytes 2097152 | tf_op jit(solution)/shard_map/reshape | solution.py:50
  138.2 2.5 copy.79
  142.1 3.6 %fusion.29 = (f32[4,16,128]{2,1,0:T(8,128)S(1)}, f32[4,16,128,136]{2,3,1,0:T(8,128)S(1)}) fusion(pred[4,128,136]{1,2,0:T(8,128)(4,1)S(1)} %or_and_fusion, bf16[1,8,16,64]{1,3,2,0:T(8,128)(2,1)S(1)} %bitcast.115, bf16[3,8,16,64]{1,3,2,0:T(8,128)(2,1)} %slice.56, bf16[4,128,16,64]{1,3,2,0:T(8,128)(2,1)} %copy.70, bf16[4,128,16,64]{3,2,1,0:T(8,128)(2,1)} %reshape.439), kind=kOutput, calls=%fused_computation.45 | convolution fusion | flops 149282816 | bytes 6721536 | tf_op jit(solution)/shard_map/gqhd,gkhd->ghqk/dot_general | solution.py:75
  148.4 2.7 %copy.80 = f32[16,4,128,64]{2,1,3,0:T(4,128)} copy(f32[16,4,128,64]{2,3,0,1:T(8,128)S(1)} %fusion.54) | data formatting | bytes 4194304 | tf_op jit(solution)/shard_map/transpose | solution.py:96
  151.2 3.1 %reshape.429 = f32[16,2,256,64]{2,1,3,0:T(2,128)S(1)} reshape(f32[16,4,128,64]{2,1,3,0:T(4,128)} %copy.80) | data formatting | bytes 4194304 | tf_op jit(solution)/shard_map/reshape | solution.py:97
  154.4 3.6 %copy.84 = bf16[2,256,16,64]{1,3,2,0:T(8,128)(2,1)} copy(bf16[2,256,16,64]{3,2,1,0:T(8,128)(2,1)} %reshape.440) | data formatting | bytes 2097152
  158.0 32.7 %all-gather = bf16[1,128,1024]{2,1,0:T(8,128)(2,1)} all-gather(bf16[1,16,1024]{2,1,0:T(8,128)(2,1)S(1)} %copy-done.6), channel_id=2, replica_groups=mesh['rec'=4,'tm'=8] {'tm'}, dimensions={1}, use_global_device_ids=true | all-gather | bytes 294912 | tf_op jit(solution)/shard_map/all_gather | solution.py:196
  191.9 32.8 %all-gather.1 = bf16[1,128,1024]{2,1,0:T(8,128)(2,1)} all-gather(bf16[1,16,1024]{2,1,0:T(8,128)(2,1)S(1)} %get-tuple-element.255), channel_id=3, replica_groups=mesh['rec'=4,'tm'=8] {'tm'}, dimensions={1}, use_global_device_ids=true | all-gather | bytes 294912 | tf_op jit(solution)/shard_map/all_gather | solution.py:197
  224.6 1.8 copy.81
  226.4 11.6 %while.15 = (s32[]{:T(128)}, f32[2,16,256]{2,1,0:T(8,128)S(1)}, f32[2,16,256,64]{2,3,1,0:T(8,128)}, f32[2,16,256]{2,0,1:T(2,128)S(1)}, f32[2,16,256]{2,0,1:T(2,1...) while((s32[]{:T(128)}, f32[2,16,256]{2,1,0:T(8,128)S(1)}, ...), condition=%wide.region_12.13_spmd.clone, body=%wide.region_9.12_spmd.clone.sunk | while | flops 141643776 | bytes 29792224 | solution.py:138
  227.2 1.7 fusion.111
  238.0 1.8 fusion.64
  241.3 2.9 %fusion.53 = bf16[512,1024]{1,0:T(8,128)(2,1)S(1)} fusion(bf16[1,512,1024]{2,1,0:T(8,128)(2,1)S(1)} %copy-done, bf16[512,1024]{0,1:T(8,128)(2,1)S(1)} %bitcast.110, bf16[1024,1024]{1,0:T(8,128)(2,1)} %all-gather.8.cloned.1.call-done, pred[512]{0:T(512)(128)(4,1)S(1)} %copy-done.14), kind=kOutput, calls=%fused_computation.72 | convolution fusion | flops 1075838976 | bytes 5243392 | tf_op jit(solution)/shard_map/dot_general | solution.py:205
  245.5 3.5 %all-to-all-start = ((bf16[8,32,1024]{2,1,0:T(8,128)(2,1)}), bf16[8,32,1024]{2,1,0:T(8,128)(2,1)S(1)}, u32[]{:S(2)}, u32[]{:S(2)}) async-start(bf16[8,32,1024]{2,1,0:T(8,128)(2,1)} %bitcast.20), calls=%async_computation | async-start | bytes 1048576 | tf_op jit(solution)/shard_map/all_to_all | solution.py:227
  249.0 10.2 %all-to-all-done = bf16[8,32,1024]{2,1,0:T(8,128)(2,1)S(1)} async-done(((bf16[8,32,1024]{2,1,0:T(8,128)(2,1)}), bf16[8,32,1024]{2,1,0:T(8,128)(2,1)S(1)}, u32[]{:S(2)}, u32[]{:S(2)}) %all-to-all-start) | async-done | bytes 524320 | tf_op jit(solution)/shard_map/all_to_all | solution.py:227
  259.2 4.4 %fusion.32 = bf16[1,1,256,2048]{3,2,1,0:T(8,128)(2,1)} fusion(bf16[256,1024]{1,0:T(8,128)(2,1)S(1)} %bitcast.111, bf16[1024,2048]{1,0:T(8,128)(2,1)} %all-gather.10.cloned.1.call-done), kind=kOutput, calls=%fused_computation.50 | convolution fusion | flops 1074266112 | bytes 5767168 | tf_op jit(solution)/shard_map/dot_general | solution.py:235
  (120 shorter events, 28.1 us)
Async XLA Ops:
  7.2 3.6 %copy-start = (bf16[1,512,1024]{2,1,0:T(8,128)(2,1)S(1)}, bf16[1,512,1024]{2,1,0:T(8,128)(2,1)}, u32[]{:S(2)}) copy-start(bf16[1,512,1024]{2,1,0:T(8,128)(2,1)} %param.11) | copy-start | bytes 3145732
  7.2 5.2 %copy-start.7 = (f32[1024]{0:T(1024)S(1)}, f32[1024]{0:T(1024)}, u32[]{:S(2)}) copy-start(f32[1024]{0:T(1024)} %param.13) | copy-start | bytes 12292
  7.2 105.1 %all-gather.6.cloned.1.call-start = ((), (), s32[]{:S(2)}) async-start(), calls=%async_computation.1 | async-start | bytes 7077888 | tf_op jit(solution)/shard_map/all_gather | solution.py:184
  7.9 233.3 %all-gather.8.cloned.1.call-start = ((), (), s32[]{:S(2)}) async-start(), calls=%async_computation.2 | async-start | bytes 2359296 | tf_op jit(solution)/shard_map/all_gather | solution.py:207
  8.7 240.3 %all-gather.10.cloned.1.call-start = ((), (), s32[]{:S(2)}) async-start(), calls=%async_computation.3 | async-start | bytes 5242880 | tf_op jit(solution)/shard_map/all_gather | solution.py:237
  9.4 6.6 %collective-permute-start = (bf16[8,1024]{1,0:T(8,128)(2,1)S(1)}, bf16[8,1024]{1,0:T(8,128)(2,1)S(1)}, u32[]{:S(2)}, u32[]{:S(2)}) collective-permute-start(bf16[8,1024]{1,0:T(8,128)(2,1)S(1)} %slice_bitcast_fusion), channel_id=1, source_target_pairs={{1,0},{2,1},{3,2},{4,3},{5,4},{6,5},{7,6},{9,8},{10,9},{11,10},{12... | collective-permute-start | bytes 49160 | tf_op jit(solution)/shard_map/ppermute | solution.py:17
  11.0 3.0 %copy-start.10 = (s32[1,1,128,1]{2,3,1,0:T(1,128)S(1)}, s32[1,1,128,1]{2,3,1,0:T(1,128)}, u32[]{:S(2)}) copy-start(s32[1,1,128,1]{2,3,1,0:T(1,128)} %param.18) | copy-start | bytes 1540
  11.4 3.5 %copy-start.11 = (s32[1,1,512]{2,1,0:T(1,128)S(1)}, s32[1,1,512]{2,1,0:T(1,128)}, u32[]{:S(2)}) copy-start(s32[1,1,512]{2,1,0:T(1,128)} %param.17) | copy-start | bytes 6148
  11.4 3.6 %copy-start.9 = (f32[1024]{0:T(1024)S(1)}, f32[1024]{0:T(1024)}, u32[]{:S(2)}) copy-start(f32[1024]{0:T(1024)} %param.14) | copy-start | bytes 12292
  119.1 2.4 copy-start.2
  145.7 1.3 copy-start.1
  154.3 3.7 %copy-start.6 = (bf16[1,16,1024]{2,1,0:T(8,128)(2,1)S(1)}, bf16[1,16,1024]{2,1,0:T(8,128)(2,1)}, u32[]{:S(2)}) copy-start(bf16[1,16,1024]{2,1,0:T(8,128)(2,1)} %get-tuple-element.256) | copy-start | bytes 98308
  154.4 72.0 %copy-start.8 = (f32[2,16,256]{2,1,0:T(8,128)S(1)}, f32[2,16,256]{2,1,0:T(8,128)}, u32[]{:S(2)}) copy-start(f32[2,16,256]{2,1,0:T(8,128)} %custom-call) | copy-start | bytes 98308
  227.2 2.9 %copy-start.3 = (f32[2,16,256,64]{2,3,1,0:T(8,128)S(1)}, f32[2,16,256,64]{2,3,1,0:T(8,128)}, u32[]{:S(2)}) copy-start(f32[2,16,256,64]{2,3,1,0:T(8,128)} %get-tuple-element.360) | copy-start | bytes 6291460 | tf_op jit(solution)/shard_map/while
  227.2 2.9 %copy-start.5 = (bf16[128,16,64]{0,2,1:T(8,128)(2,1)S(1)}, bf16[128,16,64]{0,2,1:T(8,128)(2,1)}, u32[]{:S(2)}) copy-start(bf16[128,16,64]{0,2,1:T(8,128)(2,1)} %get-tuple-element.379) | copy-start | bytes 786436 | tf_op jit(solution)/shard_map/while
  230.8 1.4 copy-start.4
  233.0 2.9 %copy-start.3 = (f32[2,16,256,64]{2,3,1,0:T(8,128)S(1)}, f32[2,16,256,64]{2,3,1,0:T(8,128)}, u32[]{:S(2)}) copy-start(f32[2,16,256,64]{2,3,1,0:T(8,128)} %get-tuple-element.360) | copy-start | bytes 6291460 | tf_op jit(solution)/shard_map/while
  233.0 2.9 %copy-start.5 = (bf16[128,16,64]{0,2,1:T(8,128)(2,1)S(1)}, bf16[128,16,64]{0,2,1:T(8,128)(2,1)}, u32[]{:S(2)}) copy-start(bf16[128,16,64]{0,2,1:T(8,128)(2,1)} %get-tuple-element.379) | copy-start | bytes 786436 | tf_op jit(solution)/shard_map/while
  236.6 1.4 copy-start.4
  239.9 1.4 copy-start.14
  241.2 2.9 %copy-start.13 = (s32[128]{0:T(128)S(1)}, s32[128]{0:T(128)}, u32[]{:S(2)}) copy-start(s32[128]{0:T(128)} %multiply_add_fusion) | copy-start | bytes 1540
  244.1 19.5 %copy-start.12 = (bf16[512,1024]{1,0:T(8,128)(2,1)}, bf16[512,1024]{1,0:T(8,128)(2,1)S(1)}, u32[]{:S(2)}) copy-start(bf16[512,1024]{1,0:T(8,128)(2,1)S(1)} %fusion.53) | copy-start | bytes 3145732
  245.5 13.7 %all-to-all-start = ((bf16[8,32,1024]{2,1,0:T(8,128)(2,1)}), bf16[8,32,1024]{2,1,0:T(8,128)(2,1)S(1)}, u32[]{:S(2)}, u32[]{:S(2)}) async-start(bf16[8,32,1024]{2,1,0:T(8,128)(2,1)} %bitcast.20), calls=%async_computation | async-start | bytes 1048576 | tf_op jit(solution)/shard_map/all_to_all | solution.py:227
Sparse Core Ops, SparseCore 0:
  10.0 102.1 all-gather.5
  114.3 48.8 all-gather.7
  164.8 32.6 all-gather.9
where the time goes:
time: 271 us; the launch traced here: 270 us
  waiting for transfers between devices  107 us (39%)
  blocking collectives  65.5 us (24%)
  local copies, waits for them, and re-layouts  41.5 us (15%)
  matrix products  25.3 us (9%)
  between operations  14.8 us (5%)
  other arithmetic  10.5 us (4%)
  starting transfers between devices  4.89 us (2%)
    all_gather x1, waiting for transfers between devices, per_device(): lax.all_gather(qkv_weight, 'tm', axis=2, tiled=True)  95.8 us
    all_gather x1, blocking collectives, per_device(): lax.all_gather(memory_values, 'tm', axis=0, tiled=True)  32.8 us
    all_gather x1, blocking collectives, per_device(): lax.all_gather(memory_keys, 'tm', axis=0, tiled=True)  32.7 us
    all_to_all x1, waiting for transfers between devices, per_device(): lax.all_to_all(sent_rows.reshape(time_count, capacity, model_width), 'tm'...  10.2 us
    dot_general x1, matrix products, per_device(): jnp.einsum('fd,kdw->kfw', stacked_rows, lax.all_gather(qkv_weight, 'tm',...  6.85 us
    reshape x2, local copies, waits for them, and re-layouts, local_part(): values[:frame_count].reshape(group_count, group_rows, head_count, head_size)  5.43 us
    reshape x2, local copies, waits for them, and re-layouts, local_part(): keys[:frame_count].reshape(group_count, group_rows, head_count, head_size)  5.42 us
  transfers between devices with their start and end apart: 5, of which 2 were waited for; matrix products, arithmetic and copies ran while one was open for 26% of the time, Pallas kernels for 0%

commit v1 on v0

--- a/solution.py
+++ b/solution.py
@@ -1,3 +1,4 @@
+import functools
 import jax
 import jax.numpy as jnp
 from jax import lax
@@ -9,6 +10,27 @@
 EPS_NORM = 1e-05
 EPS_MEMORY = 1e-06
 NEG_BIG = -1e30
+
+
+def object_divide(unit, dim_at):
+    q_next = list(unit.shape[1:])
+    q_next[dim_at] *= unit.shape[0]
+    return jnp.moveaxis(unit, 0, dim_at).reshape(q_next)
+
+
+def sides_plan(raw, net_axis, dim_k):
+    ndev = lax.axis_size(net_axis)
+    pages = [raw]
+    ledger = [(nth, (nth + 1) % ndev) for nth in range(ndev)]
+    while len(pages) < ndev:
+        pages.append(lax.ppermute(pages[-1], axis_name=net_axis, perm=ledger))
+    x_next = lax.axis_index(net_axis)
+    long_array = jnp.stack(pages)
+    pages = long_array[(x_next - jnp.arange(ndev)) % ndev]
+    return object_divide(pages, dim_k)
+
+
+show_sectors = functools.partial(sides_plan, net_axis="tm", dim_k=0)
 
 
 def shifted(block, axis, distance):
@@ -194,7 +216,7 @@
     carry = memory_update(
         carry,
         lax.all_gather(memory_keys, "tm", axis=0, tiled=True),
-        lax.all_gather(memory_values, "tm", axis=0, tiled=True),
+        show_sectors(memory_values),
         query,
         first_frame,
         length,

time: 271 us -> 291 us (1.074)
  waiting for transfers between devices: 107 us -> 142 us
  blocking collectives: 65.5 us -> 33.3 us
  local copies, waits for them, and re-layouts: 41.5 us -> 55.4 us
    ppermute x0 -> x7, waiting for transfers between devices: none -> 34.8 us  [sides_plan(): pages.append(lax.ppermute(pages[-1], axis_name=net_axis, perm=ledger))]
    all_gather x1 -> x0, blocking collectives: 32.8 us -> none  [per_device(): lax.all_gather(memory_values, 'tm', axis=0, tiled=True)]
    unnamed x26 -> x37, local copies, waits for them, and re-layouts: 4.34 us -> 10.6 us
  transfers between devices with their start and end apart: 5 -> 12, of which waited for: 2 -> 8; matrix products, arithmetic and copies ran while one was open for 26% -> 30% of each run, Pallas kernels for 0% -> 0%
where the time goes in v1:
time: 291 us; the launch traced here: 290 us
  waiting for transfers between devices  142 us (49%)
  local copies, waits for them, and re-layouts  55.4 us (19%)
  blocking collectives  33.3 us (11%)
  matrix products  26.3 us (9%)
  between operations  14.8 us (5%)
  other arithmetic  11.1 us (4%)
  starting transfers between devices  7.19 us (2%)
    all_gather x1, waiting for transfers between devices, per_device(): lax.all_gather(qkv_weight, 'tm', axis=2, tiled=True)  95.6 us
    ppermute x7, waiting for transfers between devices, sides_plan(): pages.append(lax.ppermute(pages[-1], axis_name=net_axis, perm=ledger))  34.8 us
    all_gather x1, blocking collectives, per_device(): lax.all_gather(memory_keys, 'tm', axis=0, tiled=True)  33.3 us
    unnamed x37, local copies, waits for them, and re-layouts  10.6 us
    all_to_all x1, waiting for transfers between devices, per_device(): lax.all_to_all(sent_rows.reshape(time_count, capacity, model_width), 'tm'...  10.2 us
    reshape x2, local copies, waits for them, and re-layouts, local_part(): keys[:frame_count].reshape(group_count, group_rows, head_count, head_size)  7.53 us
    dot_general x1, matrix products, per_device(): jnp.einsum('fd,kdw->kfw', stacked_rows, lax.all_gather(qkv_weight, 'tm',...  6.88 us
    reshape x2, local copies, waits for them, and re-layouts, local_part(): values[:frame_count].reshape(group_count, group_rows, head_count, head_size)  5.94 us
  transfers between devices with their start and end apart: 12, of which 8 were waited for; matrix products, arithmetic and copies ran while one was open for 30% of the time, Pallas kernels for 0%

profile of v1, /device:TPU:0, one launch (start us, length us, event | category | flops | bytes accessed | tf_op | source)
XLA Modules:
  0.0 290.3 jit_solution(3535735185126601836)
XLA Ops:
  17.1 95.6 %all-gather.5.cloned.1.call-done = bf16[3,1024,1024]{2,1,0:T(8,128)(2,1)} async-done(((bf16[3,1024,128]{2,1,0:T(8,128)(2,1)}), bf16[3,1024,1024]{2,1,0:T(8,128)(2,1)}) %all-gather.5.cloned.1.call-update) | async-done | bytes 6291472 | tf_op jit(solution)/shard_map/all_gather | solution.py:206
  112.6 6.9 %convert_bitcast_fusion = bf16[3,536,1024]{2,1,0:T(8,128)(2,1)S(1)} fusion(bf16[3,1024,1024]{2,1,0:T(8,128)(2,1)} %all-gather.5.cloned.1.call-done, bf16[16,1024]{1,0:T(8,128)(2,1)S(1)} %multiply_convert_fusion.2, bf16[8,1024]{1,0:T(8,128)(2,1)S(1)} %fusion.75, bf16[512,1024]{1,0:T(8,128)(2,1)S(1)} %multiply_convert_fusion.1), kind=kOutput, calls=%fused_computation.47 | convolution fusion | flops 3377160192 | bytes 10682368 | tf_op jit(solution)/shard_map/fd,kdw->kfw/dot_general | solution.py:203
  122.9 4.0 %reshape.492 = bf16[4,128,16,64]{3,2,1,0:T(8,128)(2,1)} reshape(bf16[1,512,1024]{2,1,0:T(8,128)(2,1)} %get-tuple-element.259) | data formatting | bytes 2097152 | tf_op jit(solution)/shard_map/reshape | solution.py:71
  126.9 3.5 %copy.70 = bf16[4,128,16,64]{1,3,2,0:T(8,128)(2,1)} copy(bf16[4,128,16,64]{3,2,1,0:T(8,128)(2,1)} %reshape.492) | data formatting | bytes 2097152 | tf_op jit(solution)/shard_map/reshape | solution.py:71
  132.5 2.3 reshape.490
  137.3 3.6 %copy.79 = bf16[4,128,16,64]{1,3,2,0:T(8,128)(2,1)} copy(bf16[4,128,16,64]{3,2,1,0:T(8,128)(2,1)} %reshape.493) | data formatting | bytes 2097152 | tf_op jit(solution)/shard_map/reshape | solution.py:72
  143.9 3.3 %fusion.29 = (f32[4,16,128]{2,1,0:T(8,128)S(1)}, f32[4,16,128,136]{2,3,1,0:T(8,128)S(1)}) fusion(pred[4,128,136]{1,2,0:T(8,128)(4,1)S(1)} %or_and_fusion, bf16[1,8,16,64]{1,3,2,0:T(8,128)(2,1)S(1)} %bitcast.131, bf16[3,8,16,64]{1,3,2,0:T(8,128)(2,1)} %slice.58, bf16[4,128,16,64]{1,3,2,0:T(8,128)(2,1)S(1)} %copy-done.1, bf16[4,128,16,64]{3,2,1,0:T(8,128)(2,1)} %reshape.490), kind=kOutput, calls=%fused_computation.46 | convolution fusion | flops 149282816 | bytes 6721536 | tf_op jit(solution)/shard_map/gqhd,gkhd->ghqk/dot_general | solution.py:97
  148.7 2.7 fusion.54
  151.4 33.3 %all-gather = bf16[1,128,1024]{2,1,0:T(8,128)(2,1)} all-gather(bf16[1,16,1024]{2,1,0:T(8,128)(2,1)S(1)} %get-tuple-element.257), channel_id=2, replica_groups=mesh['rec'=4,'tm'=8] {'tm'}, dimensions={1}, use_global_device_ids=true | all-gather | bytes 294912 | tf_op jit(solution)/shard_map/all_gather | solution.py:218
  184.7 2.3 reshape.491
  187.0 4.4 %copy.80 = f32[16,4,128,64]{2,1,3,0:T(4,128)} copy(f32[16,4,128,64]{2,3,0,1:T(8,128)} %fusion.54) | data formatting | bytes 4194304 | tf_op jit(solution)/shard_map/transpose | solution.py:118
  191.4 3.1 %reshape.475 = f32[16,2,256,64]{2,1,3,0:T(2,128)S(1)} reshape(f32[16,4,128,64]{2,1,3,0:T(4,128)} %copy.80) | data formatting | bytes 4194304 | tf_op jit(solution)/shard_map/reshape | solution.py:119
  194.7 3.6 %copy.83 = bf16[2,256,16,64]{1,3,2,0:T(8,128)(2,1)} copy(bf16[2,256,16,64]{3,2,1,0:T(8,128)(2,1)} %reshape.491) | data formatting | bytes 2097152
  201.6 4.6 %collective-permute-done.2 = bf16[16,1024]{1,0:T(8,128)(2,1)S(1)} collective-permute-done((bf16[16,1024]{1,0:T(8,128)(2,1)}, bf16[16,1024]{1,0:T(8,128)(2,1)S(1)}, u32[]{:S(2)}, u32[]{:S(2)}) %collective-permute-start.2) | collective-permute-done | bytes 32800 | tf_op jit(solution)/shard_map/ppermute | solution.py:26
  206.9 6.0 %collective-permute-done.3 = bf16[16,1024]{1,0:T(8,128)(2,1)S(1)} collective-permute-done((bf16[16,1024]{1,0:T(8,128)(2,1)S(1)}, bf16[16,1024]{1,0:T(8,128)(2,1)S(1)}, u32[]{:S(2)}, u32[]{:S(2)}) %collective-permute-start.3) | collective-permute-done | bytes 32800 | tf_op jit(solution)/shard_map/ppermute | solution.py:26
  213.5 6.0 %collective-permute-done.4 = bf16[16,1024]{1,0:T(8,128)(2,1)S(1)} collective-permute-done((bf16[16,1024]{1,0:T(8,128)(2,1)S(1)}, bf16[16,1024]{1,0:T(8,128)(2,1)S(1)}, u32[]{:S(2)}, u32[]{:S(2)}) %collective-permute-start.4) | collective-permute-done | bytes 32800 | tf_op jit(solution)/shard_map/ppermute | solution.py:26
  220.1 6.2 %collective-permute-done.5 = bf16[16,1024]{1,0:T(8,128)(2,1)S(1)} collective-permute-done((bf16[16,1024]{1,0:T(8,128)(2,1)S(1)}, bf16[16,1024]{1,0:T(8,128)(2,1)S(1)}, u32[]{:S(2)}, u32[]{:S(2)}) %collective-permute-start.5) | collective-permute-done | bytes 32800 | tf_op jit(solution)/shard_map/ppermute | solution.py:26
  227.0 6.0 %collective-permute-done.6 = bf16[16,1024]{1,0:T(8,128)(2,1)S(1)} collective-permute-done((bf16[16,1024]{1,0:T(8,128)(2,1)S(1)}, bf16[16,1024]{1,0:T(8,128)(2,1)S(1)}, u32[]{:S(2)}, u32[]{:S(2)}) %collective-permute-start.6) | collective-permute-done | bytes 32800 | tf_op jit(solution)/shard_map/ppermute | solution.py:26
  233.6 6.0 %collective-permute-done.7 = bf16[16,1024]{1,0:T(8,128)(2,1)S(1)} collective-permute-done((bf16[16,1024]{1,0:T(8,128)(2,1)S(1)}, bf16[16,1024]{1,0:T(8,128)(2,1)S(1)}, u32[]{:S(2)}, u32[]{:S(2)}) %collective-permute-start.7) | collective-permute-done | bytes 32800 | tf_op jit(solution)/shard_map/ppermute | solution.py:26
  246.6 11.6 %while.15 = (s32[]{:T(128)}, f32[2,16,256]{2,1,0:T(8,128)S(1)}, f32[2,16,256,64]{2,3,1,0:T(8,128)}, f32[2,16,256]{2,0,1:T(2,128)S(1)}, f32[2,16,256]{2,0,1:T(2,1...) while((s32[]{:T(128)}, f32[2,16,256]{2,1,0:T(8,128)S(1)}, ...), condition=%wide.region_12.13_spmd.clone, body=%wide.region_9.12_spmd.clone.sunk | while | flops 141643776 | bytes 29792224 | solution.py:160
  261.4 2.9 fusion.53
  265.6 3.5 %all-to-all-start = ((bf16[8,32,1024]{2,1,0:T(8,128)(2,1)}), bf16[8,32,1024]{2,1,0:T(8,128)(2,1)S(1)}, u32[]{:S(2)}, u32[]{:S(2)}) async-start(bf16[8,32,1024]{2,1,0:T(8,128)(2,1)} %bitcast.28), calls=%async_computation | async-start | bytes 1048576 | tf_op jit(solution)/shard_map/all_to_all | solution.py:249
  269.2 10.2 %all-to-all-done = bf16[8,32,1024]{2,1,0:T(8,128)(2,1)S(1)} async-done(((bf16[8,32,1024]{2,1,0:T(8,128)(2,1)}), bf16[8,32,1024]{2,1,0:T(8,128)(2,1)S(1)}, u32[]{:S(2)}, u32[]{:S(2)}) %all-to-all-start) | async-done | bytes 524320 | tf_op jit(solution)/shard_map/all_to_all | solution.py:249
  279.3 4.4 %fusion.32 = bf16[1,1,256,2048]{3,2,1,0:T(8,128)(2,1)} fusion(bf16[256,1024]{1,0:T(8,128)(2,1)S(1)} %bitcast.128, bf16[1024,2048]{1,0:T(8,128)(2,1)} %all-gather.9.cloned.1.call-done), kind=kOutput, calls=%fused_computation.51 | convolution fusion | flops 1074266112 | bytes 5767168 | tf_op jit(solution)/shard_map/dot_general | solution.py:257
  (148 shorter events, 50.9 us)
Async XLA Ops:
  7.2 3.6 %copy-start = (bf16[1,512,1024]{2,1,0:T(8,128)(2,1)S(1)}, bf16[1,512,1024]{2,1,0:T(8,128)(2,1)}, u32[]{:S(2)}) copy-start(bf16[1,512,1024]{2,1,0:T(8,128)(2,1)} %param.11) | copy-start | bytes 3145732
  7.2 5.3 %copy-start.8 = (f32[1024]{0:T(1024)S(1)}, f32[1024]{0:T(1024)}, u32[]{:S(2)}) copy-start(f32[1024]{0:T(1024)} %param.13) | copy-start | bytes 12292
  7.2 105.5 %all-gather.5.cloned.1.call-start = ((), (), s32[]{:S(2)}) async-start(), calls=%async_computation.1 | async-start | bytes 7077888 | tf_op jit(solution)/shard_map/all_gather | solution.py:206
  7.9 253.5 %all-gather.7.cloned.1.call-start = ((), (), s32[]{:S(2)}) async-start(), calls=%async_computation.2 | async-start | bytes 2359296 | tf_op jit(solution)/shard_map/all_gather | solution.py:229
  8.7 260.5 %all-gather.9.cloned.1.call-start = ((), (), s32[]{:S(2)}) async-start(), calls=%async_computation.3 | async-start | bytes 5242880 | tf_op jit(solution)/shard_map/all_gather | solution.py:259
  9.4 7.2 %collective-permute-start = (bf16[8,1024]{1,0:T(8,128)(2,1)S(1)}, bf16[8,1024]{1,0:T(8,128)(2,1)S(1)}, u32[]{:S(2)}, u32[]{:S(2)}) collective-permute-start(bf16[8,1024]{1,0:T(8,128)(2,1)S(1)} %slice_bitcast_fusion.1), channel_id=1, source_target_pairs={{1,0},{2,1},{3,2},{4,3},{5,4},{6,5},{7,6},{9,8},{10,9},{11,10},{12... | collective-permute-start | bytes 49160 | tf_op jit(solution)/shard_map/ppermute | solution.py:39
  11.0 3.0 %copy-start.11 = (s32[1,1,128,1]{2,3,1,0:T(1,128)S(1)}, s32[1,1,128,1]{2,3,1,0:T(1,128)}, u32[]{:S(2)}) copy-start(s32[1,1,128,1]{2,3,1,0:T(1,128)} %param.18) | copy-start | bytes 1540
  11.4 3.6 %copy-start.12 = (s32[1,1,512]{2,1,0:T(1,128)S(1)}, s32[1,1,512]{2,1,0:T(1,128)}, u32[]{:S(2)}) copy-start(s32[1,1,512]{2,1,0:T(1,128)} %param.17) | copy-start | bytes 6148
  11.4 4.3 %copy-start.10 = (f32[1024]{0:T(1024)S(1)}, f32[1024]{0:T(1024)}, u32[]{:S(2)}) copy-start(f32[1024]{0:T(1024)} %param.14) | copy-start | bytes 12292
  121.5 77.9 %collective-permute-start.1 = (bf16[16,1024]{1,0:T(8,128)(2,1)}, bf16[16,1024]{1,0:T(8,128)(2,1)}, u32[]{:S(2)}, u32[]{:S(2)}) collective-permute-start(bf16[16,1024]{1,0:T(8,128)(2,1)} %get-tuple-element.255), channel_id=1, source_target_pairs={{0,1},{1,2},{2,3},{3,4},{4,5},{5,6},{6,7},{7,0},{8,9},{9,10},{10,1... | collective-permute-start | bytes 98312 | tf_op jit(solution)/shard_map/ppermute | solution.py:26
  137.3 6.6 %copy-start.1 = (bf16[4,128,16,64]{1,3,2,0:T(8,128)(2,1)S(1)}, bf16[4,128,16,64]{1,3,2,0:T(8,128)(2,1)}, u32[]{:S(2)}) copy-start(bf16[4,128,16,64]{1,3,2,0:T(8,128)(2,1)} %copy.70) | copy-start | bytes 3145732
  198.2 48.4 %copy-start.9 = (f32[2,16,256]{2,1,0:T(8,128)S(1)}, f32[2,16,256]{2,1,0:T(8,128)}, u32[]{:S(2)}) copy-start(f32[2,16,256]{2,1,0:T(8,128)} %custom-call.3) | copy-start | bytes 98308
  199.4 6.9 %collective-permute-start.2 = (bf16[16,1024]{1,0:T(8,128)(2,1)}, bf16[16,1024]{1,0:T(8,128)(2,1)S(1)}, u32[]{:S(2)}, u32[]{:S(2)}) collective-permute-start(bf16[16,1024]{1,0:T(8,128)(2,1)} %collective-permute-done.1), channel_id=1, source_target_pairs={{0,1},{1,2},{2,3},{3,4},{4,5},{5,6},{6,7},{7,0},{8,9},{9,10},{10,1... | collective-permute-start | bytes 98312 | tf_op jit(solution)/shard_map/ppermute | solution.py:26
  206.2 6.6 %collective-permute-start.3 = (bf16[16,1024]{1,0:T(8,128)(2,1)S(1)}, bf16[16,1024]{1,0:T(8,128)(2,1)S(1)}, u32[]{:S(2)}, u32[]{:S(2)}) collective-permute-start(bf16[16,1024]{1,0:T(8,128)(2,1)S(1)} %collective-permute-done.2), channel_id=1, source_target_pairs={{0,1},{1,2},{2,3},{3,4},{4,5},{5,6},{6,7},{7,0},{8,9},{9,10},{10,1... | collective-permute-start | bytes 98312 | tf_op jit(solution)/shard_map/ppermute | solution.py:26
  212.9 6.6 %collective-permute-start.4 = (bf16[16,1024]{1,0:T(8,128)(2,1)S(1)}, bf16[16,1024]{1,0:T(8,128)(2,1)S(1)}, u32[]{:S(2)}, u32[]{:S(2)}) collective-permute-start(bf16[16,1024]{1,0:T(8,128)(2,1)S(1)} %collective-permute-done.3), channel_id=1, source_target_pairs={{0,1},{1,2},{2,3},{3,4},{4,5},{5,6},{6,7},{7,0},{8,9},{9,10},{10,1... | collective-permute-start | bytes 98312 | tf_op jit(solution)/shard_map/ppermute | solution.py:26
  219.5 6.8 %collective-permute-start.5 = (bf16[16,1024]{1,0:T(8,128)(2,1)S(1)}, bf16[16,1024]{1,0:T(8,128)(2,1)S(1)}, u32[]{:S(2)}, u32[]{:S(2)}) collective-permute-start(bf16[16,1024]{1,0:T(8,128)(2,1)S(1)} %collective-permute-done.4), channel_id=1, source_target_pairs={{0,1},{1,2},{2,3},{3,4},{4,5},{5,6},{6,7},{7,0},{8,9},{9,10},{10,1... | collective-permute-start | bytes 98312 | tf_op jit(solution)/shard_map/ppermute | solution.py:26
  226.3 6.6 %collective-permute-start.6 = (bf16[16,1024]{1,0:T(8,128)(2,1)S(1)}, bf16[16,1024]{1,0:T(8,128)(2,1)S(1)}, u32[]{:S(2)}, u32[]{:S(2)}) collective-permute-start(bf16[16,1024]{1,0:T(8,128)(2,1)S(1)} %collective-permute-done.5), channel_id=1, source_target_pairs={{0,1},{1,2},{2,3},{3,4},{4,5},{5,6},{6,7},{7,0},{8,9},{9,10},{10,1... | collective-permute-start | bytes 98312 | tf_op jit(solution)/shard_map/ppermute | solution.py:26
  232.9 6.6 %collective-permute-start.7 = (bf16[16,1024]{1,0:T(8,128)(2,1)S(1)}, bf16[16,1024]{1,0:T(8,128)(2,1)S(1)}, u32[]{:S(2)}, u32[]{:S(2)}) collective-permute-start(bf16[16,1024]{1,0:T(8,128)(2,1)S(1)} %collective-permute-done.6), channel_id=1, source_target_pairs={{0,1},{1,2},{2,3},{3,4},{4,5},{5,6},{6,7},{7,0},{8,9},{9,10},{10,1... | collective-permute-start | bytes 98312 | tf_op jit(solution)/shard_map/ppermute | solution.py:26
  247.4 2.9 %copy-start.3 = (f32[2,16,256,64]{2,3,1,0:T(8,128)S(1)}, f32[2,16,256,64]{2,3,1,0:T(8,128)}, u32[]{:S(2)}) copy-start(f32[2,16,256,64]{2,3,1,0:T(8,128)} %get-tuple-element.361) | copy-start | bytes 6291460 | tf_op jit(solution)/shard_map/while
  247.4 2.9 %copy-start.6 = (bf16[128,16,64]{0,2,1:T(8,128)(2,1)S(1)}, bf16[128,16,64]{0,2,1:T(8,128)(2,1)}, u32[]{:S(2)}) copy-start(bf16[128,16,64]{0,2,1:T(8,128)(2,1)} %get-tuple-element.380) | copy-start | bytes 786436 | tf_op jit(solution)/shard_map/while
  253.2 2.9 %copy-start.3 = (f32[2,16,256,64]{2,3,1,0:T(8,128)S(1)}, f32[2,16,256,64]{2,3,1,0:T(8,128)}, u32[]{:S(2)}) copy-start(f32[2,16,256,64]{2,3,1,0:T(8,128)} %get-tuple-element.361) | copy-start | bytes 6291460 | tf_op jit(solution)/shard_map/while
  253.2 2.9 %copy-start.6 = (bf16[128,16,64]{0,2,1:T(8,128)(2,1)S(1)}, bf16[128,16,64]{0,2,1:T(8,128)(2,1)}, u32[]{:S(2)}) copy-start(bf16[128,16,64]{0,2,1:T(8,128)(2,1)} %get-tuple-element.380) | copy-start | bytes 786436 | tf_op jit(solution)/shard_map/while
  264.3 19.4 %copy-start.14 = (bf16[512,1024]{1,0:T(8,128)(2,1)}, bf16[512,1024]{1,0:T(8,128)(2,1)S(1)}, u32[]{:S(2)}) copy-start(bf16[512,1024]{1,0:T(8,128)(2,1)S(1)} %fusion.53) | copy-start | bytes 3145732
  265.6 13.7 %all-to-all-start = ((bf16[8,32,1024]{2,1,0:T(8,128)(2,1)}), bf16[8,32,1024]{2,1,0:T(8,128)(2,1)S(1)}, u32[]{:S(2)}, u32[]{:S(2)}) async-start(bf16[8,32,1024]{2,1,0:T(8,128)(2,1)} %bitcast.28), calls=%async_computation | async-start | bytes 1048576 | tf_op jit(solution)/shard_map/all_to_all | solution.py:249
  (8 other events, 14.1 us)
Sparse Core Ops, SparseCore 0:
  10.0 102.5 all-gather.4
  114.7 50.4 all-gather.6
  166.8 32.5 all-gather.8
